TPU v7x, 32 devices: a whole 2x2x4 slice. The times are simulated.
32 devices in a mesh: tenant: 2 (over x), store: 16 (over z, y, core).
Axes of the slice: x: 2, y: 2, z: 4, core: 2. Of those that a mesh axis runs over, the one named last changes fastest.
Arguments:
- queries: bfloat16 [4096, 1024], P(('tenant', 'store')), parts along dimension 0, may hold values from -24 to 24
- own_kv: bfloat16 [4096, 256], P(('tenant', 'store')), parts along dimension 0, may hold values from -15 to 15
- store_kv: bfloat16 [1024, 256, 256], P(('tenant', 'store')), parts along dimension 0, may hold values from -15 to 15
- q_start: int32 [32], P(('tenant', 'store')), parts along dimension 0, may hold values from 12288 to 16255
- pop_ids: int32 [8], P('tenant'), parts along dimension 0, may hold values from 0 to 511
- pop_pos: int32 [32, 4], P(('tenant', 'store')), parts along dimension 0, may hold values from 0 to 12287
- rare_ids: int32 [32, 6], P(('tenant', 'store')), parts along dimension 0, may hold values from 0 to 511, as said below
- rare_count: int32 [32], P(('tenant', 'store')), parts along dimension 0, may hold values from 4 to 6, as said below
- rare_pos: int32 [32, 6], P(('tenant', 'store')), parts along dimension 0, may hold values from 0 to 12287
Outputs:
- attended: bfloat16 [4096, 1024], P(('tenant', 'store')), parts along dimension 0
There are 2 independent parts, one for each index of `tenant`. A program takes and returns all parts, laid end to end along the dimension named above; each array names one. Nothing has to cross between parts.
Inputs may be any that keep to these rules, and one draw needn't show every extreme that they name: `rare_ids`: the first rare_count entries of one device's list name blocks of different holders (id // 32); entries after them are ignored. `rare_count`: some device requests exactly 6 blocks and another exactly 4.
All inputs are finite; a program needn't handle non-finite values.
Results may differ from a plain program's by a relative error of at most 0.0085.
The roundings to bfloat16 on the way count: a program that leaves them out, or rounds other values in their place, can miss the bound.
Values may be sent and summed in bfloat16 or wider, within the bound.
A program may use at most 128 MiB of HBM per device.

v0:
```python
import jax
import jax.numpy as jnp
from jax import lax
from jax.sharding import PartitionSpec as P


def rotate(values, positions, head_size):
    half_size = head_size // 2
    freq_table = 500000.0 ** (-(2.0 * jnp.arange(half_size, dtype=jnp.float32)) / head_size)
    angles = positions.astype(jnp.float32)[:, None] * freq_table[None, :]
    cosine = jnp.cos(angles)[:, None, :]
    sine_part = jnp.sin(angles)[:, None, :]
    shaped = values.reshape(values.shape[0], -1, 2, half_size)
    first_half = shaped[:, :, 0, :]
    second_half = shaped[:, :, 1, :]
    turned = jnp.stack(
        [
            first_half * cosine - second_half * sine_part,
            second_half * cosine + first_half * sine_part,
        ],
        axis=2,
    )
    return turned.reshape(values.shape)


def block_stats(query_rows, key_rows, value_rows, allowed, scale_factor):
    scores = jnp.dot(query_rows, key_rows.T, preferred_element_type=jnp.float32) * scale_factor
    scores = jnp.where(allowed, scores, -jnp.inf)
    top_score = jnp.max(scores, axis=1)
    weights = jnp.exp(scores - top_score[:, None]).astype(jnp.bfloat16)
    weight_sum = jnp.sum(weights.astype(jnp.float32), axis=1)
    mixed_part = jnp.dot(weights, value_rows, preferred_element_type=jnp.float32)
    return (top_score, weight_sum, mixed_part)


def combine(running, top_score, weight_sum, mixed_part):
    old_top, old_sum, old_mixed = running
    peak = jnp.maximum(old_top, top_score)
    keep_factor = jnp.exp(old_top - peak)
    take_factor = jnp.exp(top_score - peak)
    return (
        peak,
        old_sum * keep_factor + weight_sum * take_factor,
        old_mixed * keep_factor[:, None] + mixed_part * take_factor[:, None],
    )


def span_fold(running, query_rows, span_kv, offset, head_size, scale_factor):
    span_len = span_kv.shape[0]
    span_keys = rotate(
        span_kv[:, :head_size].astype(jnp.float32),
        offset + jnp.arange(span_len, dtype=jnp.int32),
        head_size,
    ).astype(jnp.bfloat16)
    top_score, weight_sum, mixed_part = block_stats(
        query_rows, span_keys, span_kv[:, head_size:], True, scale_factor
    )
    return combine(running, top_score, weight_sum, mixed_part)


def body(queries, own_kv, store_kv, q_start, pop_ids, pop_pos, rare_ids, rare_count, rare_pos):
    own_index = lax.axis_index("store")
    store_count = lax.axis_size("store")
    token_count = queries.shape[0]
    head_size = own_kv.shape[1] // 2
    group_size = queries.shape[1] // head_size
    per_device = store_kv.shape[0]
    span_len = store_kv.shape[1]
    kv_width = store_kv.shape[2]
    request_most = rare_ids.shape[1]
    scale_factor = head_size ** (-0.5)
    positions = q_start[0] + jnp.arange(token_count, dtype=jnp.int32)
    query_rows = (
        rotate(queries.astype(jnp.float32), positions, head_size)
        .astype(jnp.bfloat16)
        .reshape(token_count * group_size, head_size)
    )
    own_keys = rotate(own_kv[:, :head_size].astype(jnp.float32), positions, head_size).astype(
        jnp.bfloat16
    )
    causal = (jnp.arange(token_count * group_size) // group_size)[:, None] >= jnp.arange(
        token_count
    )[None, :]
    running = block_stats(query_rows, own_keys, own_kv[:, head_size:], causal, scale_factor)
    rare_list = rare_ids[0]
    is_request = jnp.arange(request_most) < rare_count[0]
    holder_index = rare_list // per_device
    slot_index = rare_list % per_device
    match_table = (
        holder_index[:, None] == jnp.arange(store_count, dtype=jnp.int32)[None, :]
    ) & is_request[:, None]
    asked = jnp.sum(jnp.where(match_table, slot_index[:, None] + 1, 0), axis=0) - 1
    asked_pos = jnp.sum(jnp.where(match_table, rare_pos[0][:, None], 0), axis=0)
    packed = jnp.stack([asked, asked_pos], axis=1)
    incoming = lax.all_to_all(packed, "store", split_axis=0, concat_axis=0, tiled=True)
    wanted_slot = incoming[:, 0]
    reply = jnp.take(store_kv, jnp.clip(wanted_slot, 0, per_device - 1), axis=0)
    reply = jnp.where((wanted_slot >= 0)[:, None, None], reply, jnp.zeros_like(reply))
    received = lax.all_to_all(reply, "store", split_axis=0, concat_axis=0, tiled=True)
    picked = jnp.take(store_kv, pop_ids % per_device, axis=0)
    holds_it = (pop_ids // per_device == own_index)[:, None, None]
    summed = lax.psum(jnp.where(holds_it, picked.astype(jnp.float32), 0.0), "store")
    popular_kv = summed.astype(jnp.bfloat16)
    for pop_index in range(pop_ids.shape[0]):
        running = span_fold(
            running,
            query_rows,
            popular_kv[pop_index],
            pop_pos[0, pop_index],
            head_size,
            scale_factor,
        )
    rare_kv = jnp.take(received, holder_index, axis=0)
    pair_count = request_most // 2
    paired_kv = rare_kv.reshape(pair_count, 2, span_len, kv_width)
    paired_pos = rare_pos[0].reshape(pair_count, 2)
    paired_live = is_request.reshape(pair_count, 2)

    def rare_step(carry, inputs):
        pair_kv, pair_pos, pair_live = inputs
        key_pos = (pair_pos[:, None] + jnp.arange(span_len, dtype=jnp.int32)[None, :]).reshape(-1)
        flat_kv = pair_kv.reshape(2 * span_len, kv_width)
        pair_keys = (
            rotate(flat_kv[:, :head_size].astype(jnp.float32), key_pos, head_size)
            .astype(jnp.bfloat16)
            .reshape(2, span_len, head_size)
        )
        scores = (
            jnp.einsum("rd,ckd->crk", query_rows, pair_keys, preferred_element_type=jnp.float32)
            * scale_factor
        )
        top_score = jnp.max(scores, axis=2)
        weights = jnp.exp(scores - top_score[:, :, None]).astype(jnp.bfloat16)
        weight_sum = jnp.sum(weights.astype(jnp.float32), axis=2)
        mixed_part = jnp.einsum(
            "crk,ckd->crd", weights, pair_kv[:, :, head_size:], preferred_element_type=jnp.float32
        )
        top_score = jnp.where(pair_live[:, None], top_score, -jnp.inf)
        carry = combine(carry, top_score[0], weight_sum[0], mixed_part[0])
        carry = combine(carry, top_score[1], weight_sum[1], mixed_part[1])
        return (carry, None)

    running, unused_out = lax.scan(rare_step, running, (paired_kv, paired_pos, paired_live))
    final_top, final_sum, final_mixed = running
    attended = final_mixed / final_sum[:, None]
    return attended.reshape(token_count, group_size * head_size).astype(jnp.bfloat16)


def solution(mesh):
    in_specs = (
        P(("tenant", "store"), None),
        P(("tenant", "store"), None),
        P(("tenant", "store"), None, None),
        P(("tenant", "store")),
        P("tenant"),
        P(("tenant", "store"), None),
        P(("tenant", "store"), None),
        P(("tenant", "store")),
        P(("tenant", "store"), None),
    )
    out_specs = P(("tenant", "store"), None)
    return jax.shard_map(body, mesh=mesh, in_specs=in_specs, out_specs=out_specs, check_vma=False)
```

profile of v0, /device:TPU:13, one launch (start us, length us, event | category | flops | bytes accessed | tf_op | source)
XLA Modules:
  0.0 171.5 jit_solution(15668158300816286855)
XLA Ops:
  0.0 0.7 and_select_fusion.2
  1.3 0.7 select_reduce_fusion.1
  2.1 0.7 copy.49
  2.8 6.6 %all-to-all-start = ((s32[16,1,2]{2,1,0:T(1,128)}), s32[16,1,2]{2,1,0:T(1,128)S(1)}, u32[]{:S(2)}, u32[]{:S(2)}) async-start(s32[16,1,2]{2,1,0:T(1,128)} %copy.49), calls=%async_computation | async-start | bytes 16384 | tf_op jit(solution)/shard_map/all_to_all | solution.py:95
  9.3 0.7 fusion.83
  10.0 0.7 compare_and_fusion.1
  10.7 2.8 %gather_fusion = bf16[4,256,256]{2,1,0:T(8,128)(2,1)S(1)} fusion(bf16[32,256,256]{2,1,0:T(8,128)(2,1)} %param.13, s32[1024]{0:T(1024)S(1)} %pad_clamp_fusion.2), kind=kCustom, calls=%fused_computation | custom fusion | bytes 1048592 | tf_op jit(solution)/shard_map/jit(_take)/gather | solution.py:100
  13.7 55.2 %all-reduce.1 = bf16[4,256,256]{2,1,0:T(8,128)(2,1)S(1)} all-reduce(f32[4,256,256]{2,1,0:T(8,128)S(1)} %convert_select_fusion), channel_id=1, replica_groups=mesh['tenant'=2,'store'=16] {'store'}, use_global_device_ids=true, to_apply=%region_1.2 | all-reduce | flops 262144 | bytes 1572864 | tf_op jit(solution)/shard_map/psum | solution.py:102
  69.3 0.6 fusion.89
  70.0 0.6 add_convert_fusion.3
  72.7 0.6 add_convert_fusion.2
  73.8 1.2 add_convert_fusion
  75.0 0.8 fusion.60
  75.8 0.6 pad_maximum_fusion.1
  76.8 0.6 pad_maximum_fusion.4
  79.5 0.7 reshape_squeeze.3
  80.8 2.9 %gather_fusion.1 = bf16[16,256,256]{2,1,0:T(8,128)(2,1)S(1)} fusion(bf16[32,256,256]{2,1,0:T(8,128)(2,1)} %param.13, s32[1024]{0:T(1024)S(1)} %pad_clamp_fusion.1), kind=kCustom, calls=%fused_computation.1 | custom fusion | bytes 4194368 | tf_op jit(solution)/shard_map/jit(_take)/gather | solution.py:97
  83.7 2.3 %select_select_fusion = bf16[16,256,256]{2,1,0:T(8,128)(2,1)} fusion(bf16[16,256,256]{2,1,0:T(8,128)(2,1)S(1)} %gather_fusion.1, pred[16]{0:T(512)(128)(4,1)} %get-tuple-element.114, pred[16]{0:T(512)(128)(4,1)} %get-tuple-element.113), kind=kLoop, calls=%fused_computation.44 | loop fusion | flops 2097152 | bytes 4194336 | tf_op jit(solution)/shard_map/jit(_where)/select_n | solution.py:98
  85.9 22.9 %all-to-all-start.1 = ((bf16[16,256,256]{2,1,0:T(8,128)(2,1)}), bf16[16,256,256]{2,1,0:T(8,128)(2,1)}, u32[]{:S(2)}, u32[]{:S(2)}) async-start(bf16[16,256,256]{2,1,0:T(8,128)(2,1)} %select_select_fusion), calls=%async_computation.1 | async-start | bytes 4194304 | tf_op jit(solution)/shard_map/all_to_all | solution.py:99
  113.5 42.9 %all-to-all-done.1 = bf16[16,256,256]{2,1,0:T(8,128)(2,1)} async-done(((bf16[16,256,256]{2,1,0:T(8,128)(2,1)}), bf16[16,256,256]{2,1,0:T(8,128)(2,1)}, u32[]{:S(2)}, u32[]{:S(2)}) %all-to-all-start.1) | async-done | bytes 2097184 | tf_op jit(solution)/shard_map/all_to_all | solution.py:99
  156.4 2.2 %gather_fusion.2 = bf16[6,256,256]{2,1,0:T(8,128)(2,1)S(1)} fusion(bf16[16,256,256]{2,1,0:T(8,128)(2,1)} %all-to-all-done.1, s32[1024]{0:T(1024)S(1)} %pad_clamp_fusion), kind=kCustom, calls=%fused_computation.2 | custom fusion | bytes 1572888 | tf_op jit(solution)/shard_map/jit(_take)/gather | solution.py:113
  158.7 11.8 %while.14 = (s32[]{:T(128)}, f32[1024]{0:T(1024)S(1)}, f32[1024]{0:T(1024)S(1)}, f32[1024,128]{1,0:T(8,128)S(1)}, pred[3,2]{1,0:T(4,128)(4,1)S(1)}, /*index=5*/b...) while((s32[]{:T(128)}, f32[1024]{0:T(1024)S(1)}, ...), condition=%wide.region_16.17_spmd, body=%wide.region_13.16_spmd.sunk | while | flops 274902208 | bytes 13001355 | solution.py:143
  158.9 0.7 fusion.117
  160.9 0.6 fusion.122
  162.0 0.6 fusion.123
  162.9 0.7 fusion.117
  164.8 0.6 fusion.122
  165.9 0.6 fusion.123
  166.8 0.7 fusion.117
  168.7 0.6 fusion.122
  169.9 0.6 fusion.123
  170.7 0.8 convert_element_type.241
  (130 shorter events, 15.9 us)
Async XLA Ops:
  2.8 77.4 %all-to-all-start = ((s32[16,1,2]{2,1,0:T(1,128)}), s32[16,1,2]{2,1,0:T(1,128)S(1)}, u32[]{:S(2)}, u32[]{:S(2)}) async-start(s32[16,1,2]{2,1,0:T(1,128)} %copy.49), calls=%async_computation | async-start | bytes 16384 | tf_op jit(solution)/shard_map/all_to_all | solution.py:95
  13.7 55.7 %copy-start.4 = (s32[1,4]{1,0:T(1,128)S(1)}, s32[1,4]{1,0:T(1,128)}, u32[]{:S(2)}) copy-start(s32[1,4]{1,0:T(1,128)} %param.16) | copy-start | bytes 52
  13.7 57.6 %copy-start = (bf16[128,1024]{1,0:T(8,128)(2,1)S(1)}, bf16[128,1024]{1,0:T(8,128)(2,1)}, u32[]{:S(2)}) copy-start(bf16[128,1024]{1,0:T(8,128)(2,1)} %param.11) | copy-start | bytes 786436
  71.5 1.9 %slice-start = ((bf16[128,256]{1,0:T(8,128)(2,1)}), bf16[128,128]{1,0:T(8,128)(2,1)S(1)}, s32[]{:S(2)}) async-start(bf16[128,256]{1,0:T(8,128)(2,1)} %param.12), calls=%async_computation.2 | async-start | bytes 65536 | tf_op jit(solution)/shard_map/slice | solution.py:78
  71.9 6.4 %copy-start.6 = (s32[1,6]{1,0:T(1,128)S(1)}, s32[1,6]{1,0:T(1,128)}, u32[]{:S(2)}) copy-start(s32[1,6]{1,0:T(1,128)} %param.17) | copy-start | bytes 76
  71.9 6.9 %copy-start.5 = (s32[1,6]{1,0:T(1,128)S(1)}, s32[1,6]{1,0:T(1,128)}, u32[]{:S(2)}) copy-start(s32[1,6]{1,0:T(1,128)} %param.19) | copy-start | bytes 76
  85.9 23.0 %copy-start.1 = (bf16[256,1,2,64]{0,3,2,1:T(8,128)(2,1)S(1)}, bf16[256,1,2,64]{0,3,2,1:T(8,128)(2,1)}, u32[]{:S(2)}) copy-start(bf16[256,1,2,64]{0,3,2,1:T(8,128)(2,1)} %pad_maximum_fusion.1) | copy-start | bytes 196612
  85.9 70.4 %all-to-all-start.1 = ((bf16[16,256,256]{2,1,0:T(8,128)(2,1)}), bf16[16,256,256]{2,1,0:T(8,128)(2,1)}, u32[]{:S(2)}, u32[]{:S(2)}) async-start(bf16[16,256,256]{2,1,0:T(8,128)(2,1)} %select_select_fusion), calls=%async_computation.1 | async-start | bytes 4194304 | tf_op jit(solution)/shard_map/all_to_all | solution.py:99
  109.3 0.8 copy-start.2
  110.5 0.8 copy-start.3
where the time goes:
time: 172 us
  blocking collectives  55.2 us (32%)
  waiting for transfers between devices  42.9 us (25%)
  starting transfers between devices  29.4 us (17%)
  other arithmetic  19 us (11%)
  local copies, waits for them, and re-layouts  15.8 us (9%)
  matrix products  7.16 us (4%)
  between operations  1.76 us (1%)
    psum x1, blocking collectives, body(): lax.psum(jnp.where(holds_it, picked.astype(jnp.float32), 0.0), 'store')  55.2 us
    all_to_all x1, waiting for transfers between devices, body(): lax.all_to_all(reply, 'store', split_axis=0, concat_axis=0, tiled=True)  42.9 us
    all_to_all x1, starting transfers between devices, body(): lax.all_to_all(reply, 'store', split_axis=0, concat_axis=0, tiled=True)  22.9 us
    all_to_all x1, starting transfers between devices, body(): lax.all_to_all(packed, 'store', split_axis=0, concat_axis=0, tiled=True)  6.55 us
  transfers between devices with their start and end apart: 2, of which 1 were waited for; matrix products, arithmetic and copies ran while one was open for 11% of the time, Pallas kernels for 0%

commit v1 on v0

v1 whole, which is shorter than its diff:
```python
import functools

import jax
import jax.numpy as jnp
import numpy as np
from jax import lax
from jax.experimental import pallas as pl
from jax.experimental.pallas import tpu as pltpu
from jax.sharding import PartitionSpec as P

MESH = pl.DeviceIdType.MESH
INNER = 4


def kernel(
    n, per_device, requests, pops, chunk, scale,
    table_ref, pop_ref, request_ref, queries_ref, own_ref, store_hbm,
    base_cos, base_sin, step_cos, step_sin, out_ref,
    store, asks, asks_s, stage, recv, query_rows, total, tops,
    one_stage, one_recv, two_stage, two_recv, three_stage, popular,
    local_sem, ask_send, ask_recv, rare_send, rare_recv,
    one_send, one_sem, two_send, two_sem, three_send, three_sem,
):
    me = lax.axis_index("store")
    inner, outer = lax.rem(me, INNER), me // INNER
    outers = n // INNER
    head = base_cos.shape[1]
    tokens = queries_ref.shape[0]
    rows = query_rows.shape[0]
    span = stage.shape[1]
    piece = span // INNER

    def ask_copy(slot, target):
        return pltpu.make_async_remote_copy(
            src_ref=request_ref, dst_ref=asks.at[slot],
            send_sem=ask_send.at[target], recv_sem=ask_recv.at[slot],
            device_id={"store": target}, device_id_type=MESH)

    def rare_copy(slot, target):
        return pltpu.make_async_remote_copy(
            src_ref=stage.at[target], dst_ref=recv.at[slot],
            send_sem=rare_send.at[target], recv_sem=rare_recv.at[slot],
            device_id={"store": target}, device_id_type=MESH)

    def one_copy(slot, target):
        return pltpu.make_async_remote_copy(
            src_ref=one_stage.at[target], dst_ref=one_recv.at[slot],
            send_sem=one_send.at[target], recv_sem=one_sem.at[slot],
            device_id={"store": outer * INNER + target}, device_id_type=MESH)

    def two_copy(slot, target):
        return pltpu.make_async_remote_copy(
            src_ref=two_stage, dst_ref=two_recv.at[slot],
            send_sem=two_send.at[target], recv_sem=two_sem.at[slot],
            device_id={"store": target * INNER + inner}, device_id_type=MESH)

    def three_copy(slot, target):
        return pltpu.make_async_remote_copy(
            src_ref=three_stage, dst_ref=popular.at[slot],
            send_sem=three_send.at[target], recv_sem=three_sem.at[slot],
            device_id={"store": outer * INNER + target}, device_id_type=MESH)

    def peers(act):
        def step(s, carry):
            act(lax.rem(me + s, n))
            return carry
        lax.fori_loop(1, n, step, 0)

    load = pltpu.make_async_copy(store_hbm, store, local_sem.at[0])
    load.start()
    barrier = pltpu.get_barrier_semaphore()
    peers(lambda d: pl.semaphore_signal(
        barrier, inc=1, device_id={"store": d}, device_id_type=MESH))
    pl.semaphore_wait(barrier, n - 1)
    peers(lambda d: ask_copy(me, d).start())
    load.wait()

    for s in range(INNER):
        j = lax.rem(inner + s, INNER)
        begin = pl.multiple_of(j * piece, piece)
        for k in range(pops):
            part = store[lax.rem(pop_ref[k], per_device), pl.ds(begin, piece), :]
            if s == 0:
                one_recv[inner, k] = part
            else:
                one_stage[j, k] = part
        if s:
            one_copy(inner, j).start()

    cos0, sin0 = base_cos[0:1, :], base_sin[0:1, :]
    cos_n, sin_n = step_cos[:tokens, :], step_sin[:tokens, :]
    own_cos = cos0 * cos_n - sin0 * sin_n
    own_sin = sin0 * cos_n + cos0 * sin_n

    def turn(x, cosine, sine):
        x = x.astype(jnp.float32)
        return (x * cosine + pltpu.roll(x, head // 2, 1) * sine).astype(jnp.bfloat16)

    for g in range(rows // tokens):
        query_rows[g * tokens:(g + 1) * tokens, :] = turn(
            queries_ref[:, g * head:(g + 1) * head], own_cos, own_sin)

    def scores_of(at, keys):
        return lax.dot_general(
            query_rows[at, :], keys, (((1,), (1,)), ((), ())),
            preferred_element_type=jnp.float32) * scale

    def fold(block, base, live):
        cos_b, sin_b = base_cos[pl.ds(base, 1), :], base_sin[pl.ds(base, 1), :]
        cos_n, sin_n = step_cos[:span, :], step_sin[:span, :]
        keys = turn(
            block[:, :head], cos_b * cos_n - sin_b * sin_n, sin_b * cos_n + cos_b * sin_n)
        values = jnp.concatenate(
            [block[:, head:], jnp.ones((span, head), jnp.bfloat16)], axis=1)
        for c in range(rows // chunk):
            at = pl.ds(c * chunk, chunk)
            scores = scores_of(at, keys)
            top = jnp.max(scores, axis=1, keepdims=True)
            weights = jnp.exp(scores - top).astype(jnp.bfloat16)
            mixed = jnp.dot(weights, values, preferred_element_type=jnp.float32)
            top = jnp.where(live, top, -jnp.inf)
            old = tops[at, :]
            diff = top - old
            factor = jnp.exp(-jnp.abs(diff))
            rises = diff > 0.0
            keep = jnp.where(rises, factor, 1.0)
            take = jnp.where(rises, 1.0, factor)
            tops[at, :] = jnp.maximum(old, top)
            total[at, :head] = total[at, :head] * keep + mixed[:, :head] * take
            total[at, head:] = total[at, head:] * keep + mixed[:, head:] * take

    peers(lambda d: ask_copy(d, d).wait_recv())
    bring = pltpu.make_async_copy(asks, asks_s, local_sem.at[1])
    asks[me] = request_ref[...]
    bring.start()
    bring.wait()

    def slot_for(d):
        def look(r, slot):
            block_id = asks_s[d, 0, r]
            hit = (block_id // per_device == me) & (r < asks_s[d, 0, requests])
            return jnp.where(hit, lax.rem(block_id, per_device), slot)
        return lax.fori_loop(0, requests, look, jnp.int32(0), unroll=min(requests, 8))

    for s in range(1, INNER):
        j = lax.rem(inner + s, INNER)
        one_copy(j, j).wait_recv()
    for k in range(pops):
        holder = pop_ref[k] // per_device
        two_stage[k] = one_recv[lax.rem(holder, INNER), k]

    def two_start(s, carry):
        two_copy(outer, lax.rem(outer + s, outers)).start()
        return carry
    lax.fori_loop(1, outers, two_start, 0)
    two_recv[outer] = two_stage[...]

    def reply(d):
        stage[d] = store[slot_for(d)]
        rare_copy(me, d).start()
    peers(reply)
    recv[me] = store[slot_for(me)]

    own_keys = turn(own_ref[:, :head], own_cos, own_sin)
    own_values = jnp.concatenate(
        [own_ref[:, head:], jnp.ones((tokens, head), jnp.bfloat16)], axis=1)
    for c in range(rows // chunk):
        at = pl.ds(c * chunk, chunk)
        token = lax.rem(
            lax.broadcasted_iota(jnp.int32, (chunk, tokens), 0) + c * chunk, tokens)
        seen = token >= lax.broadcasted_iota(jnp.int32, (chunk, tokens), 1)
        scores = jnp.where(seen, scores_of(at, own_keys), -jnp.inf)
        top = jnp.max(scores, axis=1, keepdims=True)
        weights = jnp.exp(scores - top).astype(jnp.bfloat16)
        total[at, :] = jnp.dot(weights, own_values, preferred_element_type=jnp.float32)
        tops[at, :] = top

    def two_wait(s, carry):
        d = lax.rem(outer + s, outers)
        two_copy(d, d).wait_recv()
        return carry
    lax.fori_loop(1, outers, two_wait, 0)
    for k in range(pops):
        three_stage[k] = two_recv[pop_ref[k] // (per_device * INNER), k]
    for s in range(1, INNER):
        three_copy(inner, lax.rem(inner + s, INNER)).start()
    popular[inner] = three_stage[...]

    def rare_fold(h):
        def look(r, found):
            hit = (table_ref[r] // per_device == h) & (r < table_ref[requests])
            return jnp.where(hit, r, found)
        r = lax.fori_loop(0, requests, look, jnp.int32(-1), unroll=min(requests, 8))
        fold(recv[h], jnp.maximum(r, 0) + 1 + pops, r >= 0)

    def arrival(s, carry):
        h = lax.rem(me + n - s, n)

        @pl.when(s > 0)
        def _():
            rare_copy(h, h).wait_recv()
        rare_fold(h)
        return carry
    early = min(n, 4)
    lax.fori_loop(0, early, arrival, 0)

    for s in range(1, INNER):
        j = lax.rem(inner + s, INNER)
        three_copy(j, j).wait_recv()

    def popular_fold(k, carry):
        block = jnp.concatenate([popular[j, k] for j in range(INNER)], axis=0)
        fold(block, k + 1, True)
        return carry
    lax.fori_loop(0, pops, popular_fold, 0)
    lax.fori_loop(early, n, arrival, 0)

    for g in range(rows // tokens):
        at = pl.ds(g * tokens, tokens)
        out_ref[:, g * head:(g + 1) * head] = (
            total[at, :head] / total[at, head:]).astype(jnp.bfloat16)

    peers(lambda d: ask_copy(d, d).wait_send())
    peers(lambda d: rare_copy(d, d).wait_send())
    for s in range(1, INNER):
        j = lax.rem(inner + s, INNER)
        one_copy(j, j).wait_send()
        three_copy(j, j).wait_send()

    def two_done(s, carry):
        d = lax.rem(outer + s, outers)
        two_copy(d, d).wait_send()
        return carry
    lax.fori_loop(1, outers, two_done, 0)


def body(queries, own_kv, store_kv, q_start, pop_ids, pop_pos, rare_ids, rare_count, rare_pos):
    n = lax.axis_size("store")
    tokens = queries.shape[0]
    head = own_kv.shape[1] // 2
    rows = tokens * (queries.shape[1] // head)
    per_device, span, width = store_kv.shape
    requests = rare_ids.shape[1]
    pops = pop_ids.shape[0]
    longest = max(span, tokens)
    lanes = -(-(requests + 1) // 128) * 128
    outers = n // INNER
    piece = span // INNER

    half = np.arange(head) % (head // 2)
    freq = 500000.0 ** (-(2.0 * half) / head)
    sign = np.where(np.arange(head) < head // 2, -1.0, 1.0)
    steps = np.arange(longest)[:, None] * freq[None, :]
    step_cos = np.cos(steps).astype(np.float32)
    step_sin = (np.sin(steps) * sign).astype(np.float32)
    base = jnp.concatenate([q_start, pop_pos[0], rare_pos[0]]).astype(jnp.float32)
    angles = base[:, None] * freq.astype(np.float32)[None, :]
    base_cos = jnp.cos(angles)
    base_sin = jnp.sin(angles) * sign.astype(np.float32)[None, :]
    table = jnp.concatenate([rare_ids[0], rare_count])
    table = jnp.pad(table, (0, lanes - requests - 1))

    vmem = pl.BlockSpec(memory_space=pltpu.VMEM)
    smem = pl.BlockSpec(memory_space=pltpu.SMEM)
    dma = pltpu.SemaphoreType.DMA
    bf16 = jnp.bfloat16
    chunk = min(rows, 256)
    return pl.pallas_call(
        functools.partial(kernel, n, per_device, requests, pops, chunk, head ** -0.5),
        out_shape=jax.ShapeDtypeStruct(queries.shape, bf16),
        in_specs=[smem, smem, vmem, vmem, vmem, pl.BlockSpec(memory_space=pl.ANY)] + [vmem] * 4,
        out_specs=vmem,
        scratch_shapes=[
            pltpu.VMEM((per_device, span, width), bf16),
            pltpu.VMEM((n, 1, lanes), jnp.int32),
            pltpu.SMEM((n, 1, lanes), jnp.int32),
            pltpu.VMEM((n, span, width), bf16),
            pltpu.VMEM((n, span, width), bf16),
            pltpu.VMEM((rows, head), bf16),
            pltpu.VMEM((rows, 2 * head), jnp.float32),
            pltpu.VMEM((rows, 1), jnp.float32),
            pltpu.VMEM((INNER, pops, piece, width), bf16),
            pltpu.VMEM((INNER, pops, piece, width), bf16),
            pltpu.VMEM((pops, piece, width), bf16),
            pltpu.VMEM((outers, pops, piece, width), bf16),
            pltpu.VMEM((pops, piece, width), bf16),
            pltpu.VMEM((INNER, pops, piece, width), bf16),
            dma((2,)), dma((n,)), dma((n,)), dma((n,)), dma((n,)),
            dma((INNER,)), dma((INNER,)), dma((outers,)), dma((outers,)),
            dma((INNER,)), dma((INNER,)),
        ],
        compiler_params=pltpu.CompilerParams(
            collective_id=0, has_side_effects=True, vmem_limit_bytes=60 * 2**20),
    )(table, pop_ids, table.reshape(1, lanes), queries, own_kv, store_kv,
      base_cos, base_sin, step_cos, step_sin)


def solution(mesh):
    both = ("tenant", "store")
    in_specs = (
        P(both, None), P(both, None), P(both, None, None), P(both), P("tenant"),
        P(both, None), P(both, None), P(both), P(both, None),
    )
    return jax.shard_map(
        body, mesh=mesh, in_specs=in_specs, out_specs=P(both, None), check_vma=False)
```

time: 172 us -> 95.8 us (0.56)
  the two profiles are of different devices: /device:TPU:13 before, /device:TPU:20 now
where the time goes in v1:
time: 95.8 us; the launch traced here: 95.6 us
  Pallas kernels  89.1 us (93%)
  other arithmetic  2.87 us (3%)
  local copies, waits for them, and re-layouts  2.27 us (2%)
  between operations  1.31 us (1%)
    pallas_call x1, Pallas kernels, body(): pl.pallas_call(functools.partial(kernel, n, per_device, requests, pops, c...  89.1 us

profile of v1, /device:TPU:20, one launch (start us, length us, event | category | flops | bytes accessed | tf_op | source)
XLA Modules:
  0.0 95.6 jit_solution(14262861219083028383)
XLA Ops:
  1.3 0.7 pad_add_fusion
  2.0 0.7 add_convert_fusion
  2.8 0.6 pad_bitcast_fusion
  3.4 1.4 %fusion = (f32[11,128]{1,0:T(8,128)}, f32[11,128]{1,0:T(8,128)}) fusion(f32[128]{0:T(128)} %constant.22, f32[128]{0:T(128)} %constant.21, f32[11]{0:T(128)S(1)} %add_convert_fusion), kind=kLoop, calls=%fused_computation.2 | loop fusion | flops 2816 | bytes 12332 | tf_op jit(solution)/shard_map/mul | solution.py:259
  4.8 89.1 %shard_map.127 = bf16[128,1024]{1,0:T(8,128)(2,1)} custom-call(s32[128]{0:T(128)} %get-tuple-element.8.table_ref, s32[4]{0:T(128)} %pop_ref.1, s32[1,128]{1,0:T(1,128)} %get-tuple-element.7.request_ref, bf16[128,1024]{1,0:T(8,128)(2,1)} %queries_ref.1, bf16[128,256]{1,0:T(8,128)(2,1)} %own_ref.1, bf16[32,256,256]{2,1,0:T(8,128)(2,1)} %store_hbm.1, ...), custom_call_target="tpu_custom_call" | custom-call | tf_op jit(solution)/shard_map/pallas_call | solution.py:268
  93.9 1.7 %copy.17 = bf16[128,1024]{1,0:T(8,128)(2,1)} copy(bf16[128,1024]{1,0:T(8,128)(2,1)} %shard_map.127) | data formatting | bytes 524288

commit v2 on v1

--- a/solution.py
+++ b/solution.py
@@ -13,13 +13,13 @@
 
 
 def kernel(
-    n, per_device, requests, pops, chunk, scale,
+    n, per_device, requests, pops, chunk, power,
     table_ref, pop_ref, request_ref, queries_ref, own_ref, store_hbm,
     base_cos, base_sin, step_cos, step_sin, out_ref,
     store, asks, asks_s, stage, recv, query_rows, total, tops,
-    one_stage, one_recv, two_stage, two_recv, three_stage, popular,
+    one_stage, one_recv, two_stage, two_recv, mid_stage, three_stage, popular,
     local_sem, ask_send, ask_recv, rare_send, rare_recv,
-    one_send, one_sem, two_send, two_sem, three_send, three_sem,
+    one_send, one_sem, two_send, two_sem, mid_send, mid_sem, three_send, three_sem,
 ):
     me = lax.axis_index("store")
     inner, outer = lax.rem(me, INNER), me // INNER
@@ -50,8 +50,14 @@
 
     def two_copy(slot, target):
         return pltpu.make_async_remote_copy(
-            src_ref=two_stage, dst_ref=two_recv.at[slot],
+            src_ref=two_stage.at[target], dst_ref=two_recv.at[slot],
             send_sem=two_send.at[target], recv_sem=two_sem.at[slot],
+            device_id={"store": target * INNER + inner}, device_id_type=MESH)
+
+    def mid_copy(slot, target):
+        return pltpu.make_async_remote_copy(
+            src_ref=mid_stage, dst_ref=three_stage.at[slot],
+            send_sem=mid_send.at[target], recv_sem=mid_sem.at[slot],
             device_id={"store": target * INNER + inner}, device_id_type=MESH)
 
     def three_copy(slot, target):
@@ -100,34 +106,41 @@
         query_rows[g * tokens:(g + 1) * tokens, :] = turn(
             queries_ref[:, g * head:(g + 1) * head], own_cos, own_sin)
 
-    def scores_of(at, keys):
-        return lax.dot_general(
-            query_rows[at, :], keys, (((1,), (1,)), ((), ())),
-            preferred_element_type=jnp.float32) * scale
+    pad = total.shape[0] - head
+
+    def attend(keys, values, c, seen):
+        at = pl.ds(c * chunk, chunk)
+        scores = lax.dot_general(
+            keys, query_rows[at, :], (((1,), (1,)), ((), ())),
+            preferred_element_type=jnp.float32)
+        if seen is not None:
+            scores = jnp.where(seen, scores, -jnp.inf)
+        top = jnp.max(scores, axis=0, keepdims=True)
+        weights = jnp.exp2((scores - top) * power).astype(jnp.bfloat16)
+        return top, jnp.dot(values, weights, preferred_element_type=jnp.float32)
+
+    def flip(values):
+        return jnp.concatenate(
+            [values.T, jnp.ones((pad, values.shape[0]), jnp.bfloat16)], axis=0)
 
     def fold(block, base, live):
         cos_b, sin_b = base_cos[pl.ds(base, 1), :], base_sin[pl.ds(base, 1), :]
         cos_n, sin_n = step_cos[:span, :], step_sin[:span, :]
         keys = turn(
             block[:, :head], cos_b * cos_n - sin_b * sin_n, sin_b * cos_n + cos_b * sin_n)
-        values = jnp.concatenate(
-            [block[:, head:], jnp.ones((span, head), jnp.bfloat16)], axis=1)
+        values = flip(block[:, head:])
         for c in range(rows // chunk):
             at = pl.ds(c * chunk, chunk)
-            scores = scores_of(at, keys)
-            top = jnp.max(scores, axis=1, keepdims=True)
-            weights = jnp.exp(scores - top).astype(jnp.bfloat16)
-            mixed = jnp.dot(weights, values, preferred_element_type=jnp.float32)
+            top, mixed = attend(keys, values, c, None)
             top = jnp.where(live, top, -jnp.inf)
-            old = tops[at, :]
+            old = tops[:, at]
             diff = top - old
-            factor = jnp.exp(-jnp.abs(diff))
+            factor = jnp.exp2(-jnp.abs(diff) * power)
             rises = diff > 0.0
-            keep = jnp.where(rises, factor, 1.0)
-            take = jnp.where(rises, 1.0, factor)
-            tops[at, :] = jnp.maximum(old, top)
-            total[at, :head] = total[at, :head] * keep + mixed[:, :head] * take
-            total[at, head:] = total[at, head:] * keep + mixed[:, head:] * take
+            tops[:, at] = jnp.maximum(old, top)
+            total[:, at] = (
+                total[:, at] * jnp.where(rises, factor, 1.0)
+                + mixed * jnp.where(rises, 1.0, factor))
 
     peers(lambda d: ask_copy(d, d).wait_recv())
     bring = pltpu.make_async_copy(asks, asks_s, local_sem.at[1])
@@ -142,49 +155,31 @@
             return jnp.where(hit, lax.rem(block_id, per_device), slot)
         return lax.fori_loop(0, requests, look, jnp.int32(0), unroll=min(requests, 8))
 
+    def reply(first, last):
+        def step(s, carry):
+            d = lax.rem(me + s, n)
+            stage[d] = store[slot_for(d)]
+            rare_copy(me, d).start()
+            return carry
+        lax.fori_loop(first, last, step, 0)
+
+    cuts = [1, 3, 5, 7, n]
+    reply(cuts[0], cuts[1])
+    recv[me] = store[slot_for(me)]
+
     for s in range(1, INNER):
         j = lax.rem(inner + s, INNER)
         one_copy(j, j).wait_recv()
     for k in range(pops):
-        holder = pop_ref[k] // per_device
-        two_stage[k] = one_recv[lax.rem(holder, INNER), k]
-
-    def two_start(s, carry):
-        two_copy(outer, lax.rem(outer + s, outers)).start()
-        return carry
-    lax.fori_loop(1, outers, two_start, 0)
-    two_recv[outer] = two_stage[...]
-
-    def reply(d):
-        stage[d] = store[slot_for(d)]
-        rare_copy(me, d).start()
-    peers(reply)
-    recv[me] = store[slot_for(me)]
-
-    own_keys = turn(own_ref[:, :head], own_cos, own_sin)
-    own_values = jnp.concatenate(
-        [own_ref[:, head:], jnp.ones((tokens, head), jnp.bfloat16)], axis=1)
-    for c in range(rows // chunk):
-        at = pl.ds(c * chunk, chunk)
-        token = lax.rem(
-            lax.broadcasted_iota(jnp.int32, (chunk, tokens), 0) + c * chunk, tokens)
-        seen = token >= lax.broadcasted_iota(jnp.int32, (chunk, tokens), 1)
-        scores = jnp.where(seen, scores_of(at, own_keys), -jnp.inf)
-        top = jnp.max(scores, axis=1, keepdims=True)
-        weights = jnp.exp(scores - top).astype(jnp.bfloat16)
-        total[at, :] = jnp.dot(weights, own_values, preferred_element_type=jnp.float32)
-        tops[at, :] = top
-
-    def two_wait(s, carry):
-        d = lax.rem(outer + s, outers)
-        two_copy(d, d).wait_recv()
-        return carry
-    lax.fori_loop(1, outers, two_wait, 0)
-    for k in range(pops):
-        three_stage[k] = two_recv[pop_ref[k] // (per_device * INNER), k]
-    for s in range(1, INNER):
-        three_copy(inner, lax.rem(inner + s, INNER)).start()
-    popular[inner] = three_stage[...]
+        two_stage[k] = one_recv[lax.rem(pop_ref[k] // per_device, INNER), k]
+    for k in range(pops):
+        @pl.when(outer != k)
+        def _():
+            two_copy(outer, k).start()
+
+        @pl.when(outer == k)
+        def _():
+            two_recv[k] = two_stage[k]
 
     def rare_fold(h):
         def look(r, found):
@@ -193,16 +188,59 @@
         r = lax.fori_loop(0, requests, look, jnp.int32(-1), unroll=min(requests, 8))
         fold(recv[h], jnp.maximum(r, 0) + 1 + pops, r >= 0)
 
-    def arrival(s, carry):
-        h = lax.rem(me + n - s, n)
-
-        @pl.when(s > 0)
+    def arrivals(first, last):
+        def step(s, carry):
+            h = lax.rem(me + n - s, n)
+            rare_copy(h, h).wait_recv()
+            rare_fold(h)
+            return carry
+        lax.fori_loop(first, last, step, 0)
+
+    reply(cuts[1], cuts[2])
+
+    own_keys = turn(own_ref[:, :head], own_cos, own_sin)
+    own_values = flip(own_ref[:, head:])
+    for c in range(rows // chunk):
+        at = pl.ds(c * chunk, chunk)
+        token = lax.rem(
+            lax.broadcasted_iota(jnp.int32, (tokens, chunk), 1) + c * chunk, tokens)
+        seen = token >= lax.broadcasted_iota(jnp.int32, (tokens, chunk), 0)
+        top, total[:, at] = attend(own_keys, own_values, c, seen)
+        tops[:, at] = top
+
+    rare_fold(me)
+
+    @pl.when(outer < pops)
+    def _():
+        def two_wait(s, carry):
+            d = lax.rem(outer + s, outers)
+            pltpu.make_async_remote_copy(
+                src_ref=mid_stage, dst_ref=two_recv.at[d],
+                send_sem=mid_send.at[d], recv_sem=two_sem.at[d],
+                device_id={"store": d * INNER + inner}, device_id_type=MESH).wait_recv()
+            return carry
+        lax.fori_loop(1, outers, two_wait, 0)
+        mine = lax.rem(outer, pops)
+        mid_stage[...] = two_recv[pop_ref[mine] // (per_device * INNER)]
+
+        def mid_start(s, carry):
+            mid_copy(mine, lax.rem(outer + s, outers)).start()
+            return carry
+        lax.fori_loop(1, outers, mid_start, 0)
+        three_stage[mine] = mid_stage[...]
+
+    reply(cuts[2], cuts[3])
+    arrivals(cuts[0], cuts[1])
+    for k in range(pops):
+        @pl.when(outer != k)
         def _():
-            rare_copy(h, h).wait_recv()
-        rare_fold(h)
-        return carry
-    early = min(n, 4)
-    lax.fori_loop(0, early, arrival, 0)
+            mid_copy(k, k).wait_recv()
+    for s in range(1, INNER):
+        three_copy(inner, lax.rem(inner + s, INNER)).start()
+    for k in range(pops):
+        popular[inner, k] = three_stage[k]
+    reply(cuts[3], cuts[4])
+    arrivals(cuts[1], cuts[3])
 
     for s in range(1, INNER):
         j = lax.rem(inner + s, INNER)
@@ -213,12 +251,13 @@
         fold(block, k + 1, True)
         return carry
     lax.fori_loop(0, pops, popular_fold, 0)
-    lax.fori_loop(early, n, arrival, 0)
+
+    arrivals(cuts[3], cuts[4])
 
     for g in range(rows // tokens):
         at = pl.ds(g * tokens, tokens)
         out_ref[:, g * head:(g + 1) * head] = (
-            total[at, :head] / total[at, head:]).astype(jnp.bfloat16)
+            total[:head, at] / total[head:head + 1, at]).T.astype(jnp.bfloat16)
 
     peers(lambda d: ask_copy(d, d).wait_send())
     peers(lambda d: rare_copy(d, d).wait_send())
@@ -227,11 +266,18 @@
         one_copy(j, j).wait_send()
         three_copy(j, j).wait_send()
 
-    def two_done(s, carry):
-        d = lax.rem(outer + s, outers)
-        two_copy(d, d).wait_send()
-        return carry
-    lax.fori_loop(1, outers, two_done, 0)
+    for k in range(pops):
+        @pl.when(outer != k)
+        def _():
+            two_copy(k, k).wait_send()
+
+    @pl.when(outer < pops)
+    def _():
+        def mid_done(s, carry):
+            d = lax.rem(outer + s, outers)
+            mid_copy(lax.rem(outer, pops), d).wait_send()
+            return carry
+        lax.fori_loop(1, outers, mid_done, 0)
 
 
 def body(queries, own_kv, store_kv, q_start, pop_ids, pop_pos, rare_ids, rare_count, rare_pos):
@@ -266,7 +312,7 @@
     bf16 = jnp.bfloat16
     chunk = min(rows, 256)
     return pl.pallas_call(
-        functools.partial(kernel, n, per_device, requests, pops, chunk, head ** -0.5),
+        functools.partial(kernel, n, per_device, requests, pops, chunk, head ** -0.5 * np.log2(np.e).item()),
         out_shape=jax.ShapeDtypeStruct(queries.shape, bf16),
         in_specs=[smem, smem, vmem, vmem, vmem, pl.BlockSpec(memory_space=pl.ANY)] + [vmem] * 4,
         out_specs=vmem,
@@ -277,16 +323,17 @@
             pltpu.VMEM((n, span, width), bf16),
             pltpu.VMEM((n, span, width), bf16),
             pltpu.VMEM((rows, head), bf16),
-            pltpu.VMEM((rows, 2 * head), jnp.float32),
-            pltpu.VMEM((rows, 1), jnp.float32),
+            pltpu.VMEM((head + 16, rows), jnp.float32),
+            pltpu.VMEM((1, rows), jnp.float32),
             pltpu.VMEM((INNER, pops, piece, width), bf16),
             pltpu.VMEM((INNER, pops, piece, width), bf16),
             pltpu.VMEM((pops, piece, width), bf16),
-            pltpu.VMEM((outers, pops, piece, width), bf16),
+            pltpu.VMEM((outers, piece, width), bf16),
+            pltpu.VMEM((piece, width), bf16),
             pltpu.VMEM((pops, piece, width), bf16),
             pltpu.VMEM((INNER, pops, piece, width), bf16),
             dma((2,)), dma((n,)), dma((n,)), dma((n,)), dma((n,)),
-            dma((INNER,)), dma((INNER,)), dma((outers,)), dma((outers,)),
+            dma((INNER,)), dma((INNER,)), dma((outers,)), dma((outers,)), dma((outers,)), dma((pops,)),
             dma((INNER,)), dma((INNER,)),
         ],
         compiler_params=pltpu.CompilerParams(

time: 95.8 us -> 85.8 us (0.90)
  the two profiles are of different devices: /device:TPU:20 before, /device:TPU:27 now
where the time goes in v2:
time: 85.8 us; the launch traced here: 85.6 us
  Pallas kernels  79.2 us (92%)
  other arithmetic  2.87 us (3%)
  local copies, waits for them, and re-layouts  2.27 us (3%)
  between operations  1.31 us (2%)
    pallas_call x1, Pallas kernels, body(): pl.pallas_call(functools.partial(kernel, n, per_device, requests, pops, c...  79.2 us

profile of v2, /device:TPU:27, one launch (start us, length us, event | category | flops | bytes accessed | tf_op | source)
XLA Modules:
  0.0 85.6 jit_solution(13266697854034869544)
XLA Ops:
  1.3 0.7 pad_add_fusion
  2.0 0.7 add_convert_fusion
  2.8 0.6 pad_bitcast_fusion
  3.4 1.4 %fusion = (f32[11,128]{1,0:T(8,128)}, f32[11,128]{1,0:T(8,128)}) fusion(f32[128]{0:T(128)} %constant.22, f32[128]{0:T(128)} %constant.21, f32[11]{0:T(128)S(1)} %add_convert_fusion), kind=kLoop, calls=%fused_computation.2 | loop fusion | flops 2816 | bytes 12332 | tf_op jit(solution)/shard_map/mul | solution.py:305
  4.8 79.2 %shard_map.127 = bf16[128,1024]{1,0:T(8,128)(2,1)} custom-call(s32[128]{0:T(128)} %get-tuple-element.8.table_ref, s32[4]{0:T(128)} %pop_ref.1, s32[1,128]{1,0:T(1,128)} %get-tuple-element.7.request_ref, bf16[128,1024]{1,0:T(8,128)(2,1)} %queries_ref.1, bf16[128,256]{1,0:T(8,128)(2,1)} %own_ref.1, bf16[32,256,256]{2,1,0:T(8,128)(2,1)} %store_hbm.1, ...), custom_call_target="tpu_custom_call" | custom-call | tf_op jit(solution)/shard_map/pallas_call | solution.py:314
  83.9 1.7 %copy.17 = bf16[128,1024]{1,0:T(8,128)(2,1)} copy(bf16[128,1024]{1,0:T(8,128)(2,1)} %shard_map.127) | data formatting | bytes 524288

commit v3 on v2

--- a/solution.py
+++ b/solution.py
@@ -10,11 +10,13 @@
 
 MESH = pl.DeviceIdType.MESH
 INNER = 4
+STRIDE = 5
+WINDOW = 6
 
 
 def kernel(
     n, per_device, requests, pops, chunk, power,
-    table_ref, pop_ref, request_ref, queries_ref, own_ref, store_hbm,
+    pop_ref, request_ref, queries_ref, own_ref, store_hbm,
     base_cos, base_sin, step_cos, step_sin, out_ref,
     store, asks, asks_s, stage, recv, query_rows, total, tops,
     one_stage, one_recv, two_stage, two_recv, mid_stage, three_stage, popular,
@@ -157,13 +159,13 @@
 
     def reply(first, last):
         def step(s, carry):
-            d = lax.rem(me + s, n)
+            d = lax.rem(me + s * STRIDE, n)
             stage[d] = store[slot_for(d)]
             rare_copy(me, d).start()
             return carry
         lax.fori_loop(first, last, step, 0)
 
-    cuts = [1, 3, 5, 7, n]
+    cuts = [1, 3, 5, WINDOW + 1, n]
     reply(cuts[0], cuts[1])
     recv[me] = store[slot_for(me)]
 
@@ -183,16 +185,20 @@
 
     def rare_fold(h):
         def look(r, found):
-            hit = (table_ref[r] // per_device == h) & (r < table_ref[requests])
+            hit = (asks_s[me, 0, r] // per_device == h) & (r < asks_s[me, 0, requests])
             return jnp.where(hit, r, found)
         r = lax.fori_loop(0, requests, look, jnp.int32(-1), unroll=min(requests, 8))
         fold(recv[h], jnp.maximum(r, 0) + 1 + pops, r >= 0)
 
     def arrivals(first, last):
         def step(s, carry):
-            h = lax.rem(me + n - s, n)
+            h = lax.rem(me + (n - s) * STRIDE, n)
             rare_copy(h, h).wait_recv()
             rare_fold(h)
+
+            @pl.when(s + WINDOW < n)
+            def _():
+                reply(s + WINDOW, s + WINDOW + 1)
             return carry
         lax.fori_loop(first, last, step, 0)
 
@@ -239,7 +245,6 @@
         three_copy(inner, lax.rem(inner + s, INNER)).start()
     for k in range(pops):
         popular[inner, k] = three_stage[k]
-    reply(cuts[3], cuts[4])
     arrivals(cuts[1], cuts[3])
 
     for s in range(1, INNER):
@@ -314,7 +319,7 @@
     return pl.pallas_call(
         functools.partial(kernel, n, per_device, requests, pops, chunk, head ** -0.5 * np.log2(np.e).item()),
         out_shape=jax.ShapeDtypeStruct(queries.shape, bf16),
-        in_specs=[smem, smem, vmem, vmem, vmem, pl.BlockSpec(memory_space=pl.ANY)] + [vmem] * 4,
+        in_specs=[smem, vmem, vmem, vmem, pl.BlockSpec(memory_space=pl.ANY)] + [vmem] * 4,
         out_specs=vmem,
         scratch_shapes=[
             pltpu.VMEM((per_device, span, width), bf16),
@@ -338,7 +343,7 @@
         ],
         compiler_params=pltpu.CompilerParams(
             collective_id=0, has_side_effects=True, vmem_limit_bytes=60 * 2**20),
-    )(table, pop_ids, table.reshape(1, lanes), queries, own_kv, store_kv,
+    )(pop_ids, table.reshape(1, lanes), queries, own_kv, store_kv,
       base_cos, base_sin, step_cos, step_sin)
 
 

time: 85.8 us -> 74.6 us (0.87)
  Pallas kernels: 79.2 us -> 68 us
    pallas_call x1, Pallas kernels: 79.2 us -> 68 us  [body(): pl.pallas_call(functools.partial(kernel, n, per_device, requests, pops, c...]
where the time goes in v3:
time: 74.6 us; the launch traced here: 74.3 us
  Pallas kernels  68 us (91%)
  other arithmetic  2.87 us (4%)
  local copies, waits for them, and re-layouts  2.15 us (3%)
  between operations  1.31 us (2%)
    pallas_call x1, Pallas kernels, body(): pl.pallas_call(functools.partial(kernel, n, per_device, requests, pops, c...  68 us
    unnamed x1, local copies, waits for them, and re-layouts  1.67 us

profile of v3, /device:TPU:27, one launch (start us, length us, event | category | flops | bytes accessed | tf_op | source)
XLA Modules:
  0.0 74.3 jit_solution(11553336901667998996)
XLA Ops:
  1.3 0.7 pad_add_fusion
  2.0 0.5 pad_bitcast_fusion.request_ref
  2.5 0.7 %add_convert_fusion = f32[11]{0:T(128)S(1)} fusion(s32[6]{0:T(128)} %bitcast.5, s32[4]{0:T(128)} %bitcast.6, s32[1]{0:T(128)S(6)} %copy.15), kind=kLoop, calls=%fused_computation.4 | loop fusion | flops 33 | bytes 88 | tf_op jit(solution)/shard_map/convert_element_type | solution.py:307
  3.3 1.4 %fusion = (f32[11,128]{1,0:T(8,128)}, f32[11,128]{1,0:T(8,128)}) fusion(f32[128]{0:T(128)} %constant.22, f32[128]{0:T(128)} %constant.21, f32[11]{0:T(128)S(1)} %add_convert_fusion), kind=kLoop, calls=%fused_computation.2 | loop fusion | flops 2816 | bytes 12332 | tf_op jit(solution)/shard_map/mul | solution.py:310
  4.7 68.0 %shard_map.127 = bf16[128,1024]{1,0:T(8,128)(2,1)} custom-call(s32[4]{0:T(128)} %pop_ref.1, s32[1,128]{1,0:T(1,128)} %pad_bitcast_fusion.request_ref, bf16[128,1024]{1,0:T(8,128)(2,1)} %queries_ref.1, bf16[128,256]{1,0:T(8,128)(2,1)} %own_ref.1, bf16[32,256,256]{2,1,0:T(8,128)(2,1)} %store_hbm.1, f32[11,128]{1,0:T(8,128)} %get-tuple-element.6.base_cos, ...), custom_call_target="tpu_custom_call" | custom-call | tf_op jit(solution)/shard_map/pallas_call | solution.py:319
  72.7 1.7 %copy.17 = bf16[128,1024]{1,0:T(8,128)(2,1)} copy(bf16[128,1024]{1,0:T(8,128)(2,1)} %shard_map.127) | data formatting | bytes 524288

commit v4 on v3

--- a/solution.py
+++ b/solution.py
@@ -11,7 +11,7 @@
 MESH = pl.DeviceIdType.MESH
 INNER = 4
 STRIDE = 5
-WINDOW = 6
+WINDOW = 7
 
 
 def kernel(
@@ -315,7 +315,7 @@
     smem = pl.BlockSpec(memory_space=pltpu.SMEM)
     dma = pltpu.SemaphoreType.DMA
     bf16 = jnp.bfloat16
-    chunk = min(rows, 256)
+    chunk = min(rows, 512)
     return pl.pallas_call(
         functools.partial(kernel, n, per_device, requests, pops, chunk, head ** -0.5 * np.log2(np.e).item()),
         out_shape=jax.ShapeDtypeStruct(queries.shape, bf16),

time: 74.6 us -> 73 us (0.979)
  Pallas kernels: 68 us -> 65.8 us
    pallas_call x1, Pallas kernels: 68 us -> 65.8 us  [body(): pl.pallas_call(functools.partial(kernel, n, per_device, requests, pops, c...]
where the time goes in v4:
time: 73 us; the launch traced here: 72.1 us
  Pallas kernels  65.8 us (90%)
  other arithmetic  2.87 us (4%)
  local copies, waits for them, and re-layouts  2.15 us (3%)
  between operations  1.31 us (2%)
    pallas_call x1, Pallas kernels, body(): pl.pallas_call(functools.partial(kernel, n, per_device, requests, pops, c...  65.8 us
    unnamed x1, local copies, waits for them, and re-layouts  1.67 us

profile of v4, /device:TPU:27, one launch (start us, length us, event | category | flops | bytes accessed | tf_op | source)
XLA Modules:
  0.0 72.1 jit_solution(1585344464003390866)
XLA Ops:
  1.3 0.7 %pad_add_fusion = s32[7]{0:T(128)S(1)} fusion(s32[1]{0:T(128)S(6)} %copy.16, s32[6]{0:T(128)} %bitcast.7), kind=kLoop, calls=%fused_computation.3 | loop fusion | flops 7 | bytes 56 | tf_op jit(solution)/shard_map/concatenate | solution.py:311
  2.0 0.5 pad_bitcast_fusion.request_ref
  2.5 0.7 %add_convert_fusion = f32[11]{0:T(128)S(1)} fusion(s32[6]{0:T(128)} %bitcast.5, s32[4]{0:T(128)} %bitcast.6, s32[1]{0:T(128)S(6)} %copy.15), kind=kLoop, calls=%fused_computation.4 | loop fusion | flops 33 | bytes 88 | tf_op jit(solution)/shard_map/convert_element_type | solution.py:307
  3.3 1.4 %fusion = (f32[11,128]{1,0:T(8,128)}, f32[11,128]{1,0:T(8,128)}) fusion(f32[128]{0:T(128)} %constant.22, f32[128]{0:T(128)} %constant.21, f32[11]{0:T(128)S(1)} %add_convert_fusion), kind=kLoop, calls=%fused_computation.2 | loop fusion | flops 2816 | bytes 12332 | tf_op jit(solution)/shard_map/mul | solution.py:310
  4.7 65.8 %shard_map.127 = bf16[128,1024]{1,0:T(8,128)(2,1)} custom-call(s32[4]{0:T(128)} %pop_ref.1, s32[1,128]{1,0:T(1,128)} %pad_bitcast_fusion.request_ref, bf16[128,1024]{1,0:T(8,128)(2,1)} %queries_ref.1, bf16[128,256]{1,0:T(8,128)(2,1)} %own_ref.1, bf16[32,256,256]{2,1,0:T(8,128)(2,1)} %store_hbm.1, f32[11,128]{1,0:T(8,128)} %get-tuple-element.6.base_cos, ...), custom_call_target="tpu_custom_call" | custom-call | tf_op jit(solution)/shard_map/pallas_call | solution.py:319
  70.5 1.7 %copy.17 = bf16[128,1024]{1,0:T(8,128)(2,1)} copy(bf16[128,1024]{1,0:T(8,128)(2,1)} %shard_map.127) | data formatting | bytes 524288
